TPU v7x, 256 devices: a whole 4x4x8 slice. The times are simulated.
256 devices in a mesh: dp: 4 (over x), blk: 16 (over z_lo, y, core), mp: 4 (over z_hi).
Axes of the slice: x: 4, y: 4, z: 8 (z_hi: 4, z_lo: 2; z = z_hi * 2 + z_lo), core: 2. Of those that a mesh axis runs over, the one named last changes fastest.
Arguments:
- tokens: bfloat16 [16384, 7168], P('dp', ('blk', 'mp')), may hold values from -6 to 6
- trainer_q: float32 [3584, 7168], P(('mp', 'blk'), 'dp'), may hold values from -0.0625 to 0.0625
- kv_pool: bfloat16 [2, 8192, 3584], P(None, ('dp', 'blk'), 'mp')
- prompt_kv: bfloat16 [2, 16384, 3584], P(None, ('dp', 'blk'), 'mp'), may hold values from -15 to 15
- page_table: int32 [64, 64], P(('dp', 'blk')), may hold values from 0 to 127, as said below
- page_count: int32 [64], P(('dp', 'blk')), may hold values from 1 to 64
- prompt_len: int32 [64], P(('dp', 'blk')), may hold values from 64 to 256
Outputs:
- server_q: bfloat16 [3584, 7168], P('mp', 'blk')
- attn_out: bfloat16 [16384, 3584], P(('dp', 'blk'), 'mp')
Inputs may be any that keep to these rules, and one draw needn't show every extreme that they name: `page_table`: the entries of a row are distinct page numbers of the request's group.
All inputs are finite; a program needn't handle non-finite values.
Results may differ from a plain program's by a relative error of at most 0.012.
The roundings to bfloat16 on the way count: a program that leaves them out, or rounds other values in their place, can miss the bound.
Values may be sent and summed in bfloat16 or wider, within the bound.
A program may use at most 128 MiB of HBM per device.

v0:
```python
import jax
import jax.numpy as jnp
from jax import lax
from jax.sharding import PartitionSpec as P

HD = 224
PAGE = 16


def attend_block(softmax_state, query_heads, key_heads, value_heads, key_mask):
    running_max, row_total, weighted = softmax_state
    scores = jnp.einsum(
        "thd,khd->htk", query_heads, key_heads, preferred_element_type=jnp.float32
    ) * HD ** (-0.5)
    scores = jnp.where(key_mask[None], scores, -1e30)
    new_max = jnp.maximum(running_max, jnp.max(scores, axis=2))
    weights = jnp.where(key_mask[None], jnp.exp(scores - new_max[:, :, None]), 0.0)
    factor = jnp.exp(running_max - new_max)
    row_total = row_total * factor + jnp.sum(weights, axis=2)
    weighted = weighted * factor[:, :, None] + jnp.einsum(
        "htk,khd->htd",
        weights.astype(jnp.bfloat16),
        value_heads,
        preferred_element_type=jnp.float32,
    )
    return (new_max, row_total, weighted)


def body(tokens, trainer_q, kv_pool, prompt_kv, page_table, page_count, prompt_len):
    trainer_rows = lax.all_gather(trainer_q.astype(jnp.bfloat16), "dp", axis=1, tiled=True)
    server_q = lax.all_to_all(trainer_rows, "blk", split_axis=1, concat_axis=0, tiled=True)
    features = lax.all_gather(tokens, "mp", axis=1, tiled=True)
    own_rows = features.shape[0] // lax.axis_size("blk")
    head_width = server_q.shape[0]
    token_local = lax.all_to_all(features, "blk", split_axis=0, concat_axis=1, tiled=True)
    queries = jnp.einsum(
        "td,hd->th",
        token_local,
        lax.all_gather(server_q, "blk", axis=1, tiled=True),
        preferred_element_type=jnp.float32,
    )
    queries = queries.astype(jnp.bfloat16)
    head_count = head_width // HD
    query_heads = queries.reshape(own_rows, head_count, HD)
    length = prompt_len[0]
    row_pages = page_table[0]
    live_slots = jnp.arange(row_pages.shape[0], dtype=jnp.int32) < page_count[0]
    row_index = jnp.arange(own_rows, dtype=jnp.int32)
    own_mask = (row_index[None, :] <= row_index[:, None]) & (row_index[None, :] < length)
    softmax_state = (
        jnp.full((head_count, own_rows), -1e30, jnp.float32),
        jnp.zeros((head_count, own_rows), jnp.float32),
        jnp.zeros((head_count, own_rows, HD), jnp.float32),
    )
    softmax_state = attend_block(
        softmax_state,
        query_heads,
        prompt_kv[0].reshape(own_rows, head_count, HD),
        prompt_kv[1].reshape(own_rows, head_count, HD),
        own_mask,
    )
    shard_piece = lax.all_gather(kv_pool, "blk", axis=1, tiled=True)
    key_count = shard_piece.shape[1]
    page_ids = jnp.arange(key_count, dtype=jnp.int32) // PAGE
    page_used = jnp.any((row_pages[None, :] == page_ids[:, None]) & live_slots[None, :], axis=1)
    key_mask = jnp.broadcast_to(page_used[None, :], (own_rows, key_count))
    running_max, row_total, weighted = attend_block(
        softmax_state,
        query_heads,
        shard_piece[0].reshape(key_count, head_count, HD),
        shard_piece[1].reshape(key_count, head_count, HD),
        key_mask,
    )
    mixed = weighted / row_total[:, :, None]
    mixed = jnp.where((row_index < length)[None, :, None], mixed, 0.0)
    mixed = jnp.transpose(mixed, (1, 0, 2)).reshape(own_rows, head_width).astype(jnp.bfloat16)
    return (server_q, mixed)


def solution(mesh):
    in_specs = (
        P("dp", ("blk", "mp")),
        P(("mp", "blk"), "dp"),
        P(None, ("dp", "blk"), "mp"),
        P(None, ("dp", "blk"), "mp"),
        P(("dp", "blk"), None),
        P(("dp", "blk")),
        P(("dp", "blk")),
    )
    out_specs = (P("mp", "blk"), P(("dp", "blk"), "mp"))
    return jax.shard_map(body, mesh=mesh, in_specs=in_specs, out_specs=out_specs, check_vma=False)
```

profile of v0, /device:TPU:1, one launch (start us, length us, event | category | flops | bytes accessed | tf_op | source)
XLA Modules:
  0.0 293.7 jit_solution(181580022779690303)
XLA Ops:
  7.2 0.7 all-gather.4.cloned.1.call-update
  7.9 0.7 all-gather.8.cloned.1.call-update
  8.7 1.0 convert_element_type.18
  9.7 13.0 %all_gather.12 = bf16[56,7168]{1,0:T(8,128)(2,1)S(1)} all-gather(bf16[56,1792]{1,0:T(8,128)(2,1)S(1)} %convert_element_type.18), channel_id=1, replica_groups=mesh['dp'=4,'blk'=16,'mp'=4] {'dp'}, dimensions={1}, use_global_device_ids=true | all-gather | bytes 1003520 | tf_op jit(solution)/shard_map/all_gather | solution.py:30
  22.7 1.1 all_to_all.28
  23.8 0.5 copy.48
  24.3 50.4 %all_to_all.38 = bf16[56,16,448]{2,0,1:T(8,128)(2,1)S(1)} all-to-all(bf16[56,16,448]{2,0,1:T(8,128)(2,1)S(1)} %copy.48), channel_id=1, replica_groups=mesh['dp'=4,'blk'=16,'mp'=4] {'blk'}, dimensions={1} | all-to-all | bytes 1605632 | tf_op jit(solution)/shard_map/all_to_all | solution.py:31
  74.7 1.2 copy.57
  76.0 24.8 %all-gather.4.cloned.1.call-done = bf16[4096,448]{0,1:T(8,128)(2,1)} async-done(((bf16[4096,112]{0,1:T(8,128)(2,1)}), bf16[4096,448]{0,1:T(8,128)(2,1)}) %all-gather.4.cloned.1.call-update) | async-done | bytes 3670032 | tf_op jit(solution)/shard_map/all_gather | solution.py:32
  100.8 4.3 %copy.62 = bf16[56,16,8,256]{3,2,0,1:T(8,128)(2,1)} copy(bf16[56,16,8,256]{3,2,1,0:T(8,128)(2,1)} %bitcast.70) | data formatting | bytes 7340032 | tf_op jit(solution)/shard_map/all_to_all | solution.py:35
  105.1 5.0 %all-to-all-start.1 = ((bf16[16,256,448]{1,2,0:T(8,128)(2,1)}), bf16[16,256,448]{1,2,0:T(8,128)(2,1)}, u32[]{:S(2)}, u32[]{:S(2)}) async-start(bf16[16,256,448]{1,2,0:T(8,128)(2,1)} %bitcast.66), calls=%async_computation.1 | async-start | bytes 7340032 | tf_op jit(solution)/shard_map/all_to_all | solution.py:35
  111.7 0.2 copy.53
  112.3 76.3 %all-gather.8.cloned.1.call-done = bf16[2,2048,896]{2,1,0:T(8,128)(2,1)} async-done(((bf16[2,128,896]{2,1,0:T(8,128)(2,1)}), bf16[2,2048,896]{2,1,0:T(8,128)(2,1)}) %all-gather.8.cloned.1.call-update) | async-done | bytes 7340048 | tf_op jit(solution)/shard_map/all_gather | solution.py:62
  188.6 6.8 %fusion.36 = (bf16[1,2048,896]{2,1,0:T(8,128)(2,1)}, bf16[1,2048,896]{2,1,0:T(8,128)(2,1)}) fusion(bf16[2,2048,896]{2,1,0:T(8,128)(2,1)} %all-gather.8.cloned.1.call-done), kind=kLoop, calls=%fused_computation.51 | loop fusion | bytes 14680064 | tf_op jit(solution)/shard_map/slice | solution.py:70
  195.3 6.2 %copy.55 = bf16[1,2048,896]{1,2,0:T(8,128)(2,1)} copy(bf16[1,2048,896]{2,1,0:T(8,128)(2,1)} %get-tuple-element.14) | data formatting | bytes 7340032 | tf_op jit(solution)/shard_map/slice | solution.py:70
  201.5 6.2 %copy.56 = bf16[1,2048,896]{1,2,0:T(8,128)(2,1)} copy(bf16[1,2048,896]{2,1,0:T(8,128)(2,1)} %get-tuple-element.15) | data formatting | bytes 7340032 | tf_op jit(solution)/shard_map/slice | solution.py:71
  207.7 59.1 %all-gather.6.cloned.1.call-done = bf16[896,7168]{0,1:T(8,128)(2,1)} async-done(((bf16[896,448]{0,1:T(8,128)(2,1)}), bf16[896,7168]{0,1:T(8,128)(2,1)}) %all-gather.6.cloned.1.call-update) | async-done | bytes 12845072 | tf_op jit(solution)/shard_map/all_gather | solution.py:39
  266.8 9.8 %convolution_convert_fusion = bf16[256,896]{1,0:T(8,128)(2,1)S(1)} fusion(bf16[256,7168]{0,1:T(8,128)(2,1)} %bitcast.4, bf16[896,7168]{0,1:T(8,128)(2,1)} %all-gather.6.cloned.1.call-done), kind=kOutput, calls=%fused_computation.17 | convolution fusion | flops 3288563712 | bytes 16973824 | tf_op jit(solution)/shard_map/td,hd->th/dot_general | solution.py:36
  276.8 0.4 fusion.38
  277.2 4.0 %fusion = (f32[4,256]{1,0:T(4,128)S(1)}, f32[4,256,2048]{2,1,0:T(8,128)S(1)}) fusion(pred[2048]{0:T(1024)(128)(4,1)S(1)} %and_reduce_fusion, bf16[256,4,224]{0,2,1:T(8,128)(2,1)S(1)} %bitcast.69, bf16[2048,4,224]{0,2,1:T(8,128)(2,1)} %bitcast.67), kind=kOutput, calls=%fused_computation.2 | convolution fusion | flops 945814528 | bytes 12523520 | tf_op jit(solution)/shard_map/thd,khd->htk/dot_general | solution.py:12
  281.2 2.2 fusion.1
  283.4 2.1 fusion.7
  285.8 0.4 fusion.15
  286.2 1.0 copy.58
  (22 shorter events, 1.2 us)
Async XLA Ops:
  7.2 93.6 %all-gather.4.cloned.1.call-start = ((), (), s32[]{:S(2)}) async-start(), calls=%async_computation.2 | async-start | bytes 4587520 | tf_op jit(solution)/shard_map/all_gather | solution.py:32
  7.9 180.7 %all-gather.8.cloned.1.call-start = ((), (), s32[]{:S(2)}) async-start(), calls=%async_computation.4 | async-start | bytes 7798784 | tf_op jit(solution)/shard_map/all_gather | solution.py:62
  8.6 258.2 %all-gather.6.cloned.1.call-start = ((), (), s32[]{:S(2)}) async-start(), calls=%async_computation.3 | async-start | bytes 13647872 | tf_op jit(solution)/shard_map/all_gather | solution.py:39
  74.7 36.1 %copy-start.1 = (bf16[2,256,896]{2,1,0:T(8,128)(2,1)S(1)}, bf16[2,256,896]{2,1,0:T(8,128)(2,1)}, u32[]{:S(2)}) copy-start(bf16[2,256,896]{2,1,0:T(8,128)(2,1)} %param.10) | copy-start | bytes 2752516
  100.8 11.2 %copy-start.2 = (s32[1,64]{1,0:T(1,128)S(1)}, s32[1,64]{1,0:T(1,128)}, u32[]{:S(2)}) copy-start(s32[1,64]{1,0:T(1,128)} %param.11) | copy-start | bytes 772
  105.1 102.6 %all-to-all-start.1 = ((bf16[16,256,448]{1,2,0:T(8,128)(2,1)}), bf16[16,256,448]{1,2,0:T(8,128)(2,1)}, u32[]{:S(2)}, u32[]{:S(2)}) async-start(bf16[16,256,448]{1,2,0:T(8,128)(2,1)} %bitcast.66), calls=%async_computation.1 | async-start | bytes 7340032 | tf_op jit(solution)/shard_map/all_to_all | solution.py:35
  277.2 6.2 %copy-start = (bf16[1,2048,896]{1,2,0:T(8,128)(2,1)S(1)}, bf16[1,2048,896]{1,2,0:T(8,128)(2,1)}, u32[]{:S(2)}) copy-start(bf16[1,2048,896]{1,2,0:T(8,128)(2,1)} %copy.56) | copy-start | bytes 11010052
Sparse Core Ops, SparseCore 0:
  9.8 90.9 all-gather.3
  102.6 85.9 all-gather.7
  191.0 75.7 all-gather.5
where the time goes:
time: 294 us
  waiting for transfers between devices  162 us (55%)
  blocking collectives  63.4 us (22%)
  local copies, waits for them, and re-layouts  28 us (10%)
  matrix products  16.6 us (6%)
  between operations  15.2 us (5%)
  starting transfers between devices  5.13 us (2%)
  other arithmetic  3.74 us (1%)
    all_gather x1, waiting for transfers between devices, body(): shard_piece = lax.all_gather(kv_pool, 'blk', axis=1, tiled=True)  76.3 us
    all_gather x1, waiting for transfers between devices, body(): lax.all_gather(server_q, 'blk', axis=1, tiled=True)  59.1 us
    all_to_all x1, blocking collectives, body(): lax.all_to_all(trainer_rows, 'blk', split_axis=1, concat_axis=0, tiled=True)  50.4 us
    all_gather x1, waiting for transfers between devices, body(): features = lax.all_gather(tokens, 'mp', axis=1, tiled=True)  24.8 us
    all_gather x1, blocking collectives, body(): lax.all_gather(trainer_q.astype(jnp.bfloat16), 'dp', axis=1, tiled=True)  13 us
    slice x2, local copies, waits for them, and re-layouts, body(): shard_piece[0].reshape(key_count, head_count, HD)  12.9 us
    dot_general x1, matrix products, body(): jnp.einsum('td,hd->th', token_local, lax.all_gather(server_q, 'blk', axis...  9.77 us
    slice x1, local copies, waits for them, and re-layouts, body(): shard_piece[1].reshape(key_count, head_count, HD)  6.2 us
  transfers between devices with their start and end apart: 4, of which 3 were waited for; matrix products, arithmetic and copies ran while one was open for 9% of the time, Pallas kernels for 0%

commit v1 on v0

--- a/solution.py
+++ b/solution.py
@@ -5,6 +5,11 @@
 
 HD = 224
 PAGE = 16
+
+
+def exchange_gather(x, axis, d):
+    outgoing = jnp.stack([x] * lax.axis_size(axis))
+    return jnp.concatenate(lax.all_to_all(outgoing, axis, 0, 0), axis=d)
 
 
 def attend_block(softmax_state, query_heads, key_heads, value_heads, key_mask):
@@ -36,7 +41,7 @@
     queries = jnp.einsum(
         "td,hd->th",
         token_local,
-        lax.all_gather(server_q, "blk", axis=1, tiled=True),
+        exchange_gather(server_q, "blk", 1),
         preferred_element_type=jnp.float32,
     )
     queries = queries.astype(jnp.bfloat16)

time: 294 us -> 405 us (1.38)
  waiting for transfers between devices: 162 us -> 293 us
  blocking collectives: 63.4 us -> 13 us
  starting transfers between devices: 5.13 us -> 24.4 us
  local copies, waits for them, and re-layouts: 28 us -> 34.8 us
    all_gather x1, waiting for transfers between devices: 76.3 us -> 177 us  [body(): shard_piece = lax.all_gather(kv_pool, 'blk', axis=1, tiled=True)]
    all_gather x1 -> x0, waiting for transfers between devices: 59.1 us -> none  [body(): lax.all_gather(server_q, 'blk', axis=1, tiled=True)]
    all_to_all x1 -> x0, blocking collectives: 50.4 us -> none  [body(): lax.all_to_all(trainer_rows, 'blk', split_axis=1, concat_axis=0, tiled=True)]
    all_to_all x1, waiting for transfers between devices: 0.01 us -> 46.9 us  [body(): lax.all_to_all(features, 'blk', split_axis=0, concat_axis=1, tiled=True)]
    all_gather x1, waiting for transfers between devices: 24.8 us -> 68.3 us  [body(): features = lax.all_gather(tokens, 'mp', axis=1, tiled=True)]
    all_to_all x0 -> x2, starting transfers between devices: none -> 19.1 us  [the longest x1 11.1 us: exchange_gather(): return jnp.concatenate(lax.all_to_all(outgoing, axis, 0, 0), axis=d)]
    another operation x0 -> x1, local copies, waits for them, and re-layouts: none -> 6.38 us  [exchange_gather(): outgoing = jnp.stack([x] * lax.axis_size(axis))]
  transfers between devices with their start and end apart: 4 -> 5, of which waited for: 3 -> 3; matrix products, arithmetic and copies ran while one was open for 9% -> 7% of each run, Pallas kernels for 0% -> 0%
where the time goes in v1:
time: 405 us; the launch traced here: 403 us
  waiting for transfers between devices  293 us (72%)
  local copies, waits for them, and re-layouts  34.8 us (9%)
  starting transfers between devices  24.4 us (6%)
  between operations  16.9 us (4%)
  matrix products  16.6 us (4%)
  blocking collectives  13 us (3%)
    all_gather x1, waiting for transfers between devices, body(): shard_piece = lax.all_gather(kv_pool, 'blk', axis=1, tiled=True)  177 us
    all_gather x1, waiting for transfers between devices, body(): features = lax.all_gather(tokens, 'mp', axis=1, tiled=True)  68.3 us
    all_to_all x1, waiting for transfers between devices, body(): lax.all_to_all(features, 'blk', split_axis=0, concat_axis=1, tiled=True)  46.9 us
    all_gather x1, blocking collectives, body(): lax.all_gather(trainer_q.astype(jnp.bfloat16), 'dp', axis=1, tiled=True)  13 us
    slice x2, local copies, waits for them, and re-layouts, body(): shard_piece[0].reshape(key_count, head_count, HD)  13 us
    all_to_all x1, starting transfers between devices, exchange_gather(): return jnp.concatenate(lax.all_to_all(outgoing, axis, 0, 0), axis=d)  11.1 us
    dot_general x1, matrix products, body(): jnp.einsum('td,hd->th', token_local, exchange_gather(server_q, 'blk', 1),...  9.77 us
  transfers between devices with their start and end apart: 5, of which 3 were waited for; matrix products, arithmetic and copies ran while one was open for 7% of the time, Pallas kernels for 0%

profile of v1, /device:TPU:1, one launch (start us, length us, event | category | flops | bytes accessed | tf_op | source)
XLA Modules:
  0.0 402.6 jit_solution(17168457145344901552)
XLA Ops:
  8.0 0.7 all-gather.3.cloned.1.call-update
  8.7 1.0 convert_element_type.18
  9.8 13.0 %all_gather.9 = bf16[56,7168]{1,0:T(8,128)(2,1)S(1)} all-gather(bf16[56,1792]{1,0:T(8,128)(2,1)S(1)} %convert_element_type.18), channel_id=1, replica_groups=mesh['dp'=4,'blk'=16,'mp'=4] {'dp'}, dimensions={1}, use_global_device_ids=true | all-gather | bytes 1003520 | tf_op jit(solution)/shard_map/all_gather | solution.py:35
  22.7 1.1 all_to_all.29
  23.8 1.4 copy.29
  25.3 8.1 %all-to-all-start = ((bf16[56,16,448]{2,0,1:T(8,128)(2,1)}), bf16[56,16,448]{2,0,1:T(8,128)(2,1)S(1)}, u32[]{:S(2)}, u32[]{:S(2)}) async-start(bf16[56,16,448]{2,0,1:T(8,128)(2,1)} %copy.29), calls=%async_computation | async-start | bytes 1835008 | tf_op jit(solution)/shard_map/all_to_all | solution.py:36
  33.3 68.3 %all-gather.3.cloned.1.call-done = bf16[4096,448]{0,1:T(8,128)(2,1)} async-done(((bf16[4096,112]{0,1:T(8,128)(2,1)}), bf16[4096,448]{0,1:T(8,128)(2,1)}) %all-gather.3.cloned.1.call-update) | async-done | bytes 3670032 | tf_op jit(solution)/shard_map/all_gather | solution.py:37
  101.6 4.2 %copy.43 = bf16[56,16,8,256]{3,2,0,1:T(8,128)(2,1)} copy(bf16[56,16,8,256]{3,2,1,0:T(8,128)(2,1)} %bitcast.84) | data formatting | bytes 7340032 | tf_op jit(solution)/shard_map/all_to_all | solution.py:40
  105.8 5.0 %all-to-all-start.1 = ((bf16[16,256,448]{1,2,0:T(8,128)(2,1)}), bf16[16,256,448]{1,2,0:T(8,128)(2,1)}, u32[]{:S(2)}, u32[]{:S(2)}) async-start(bf16[16,256,448]{1,2,0:T(8,128)(2,1)} %bitcast.79), calls=%async_computation.1 | async-start | bytes 7340032 | tf_op jit(solution)/shard_map/all_to_all | solution.py:40
  110.8 0.8 copy.38
  111.7 46.9 %all-to-all-done.1 = bf16[16,256,448]{1,2,0:T(8,128)(2,1)} async-done(((bf16[16,256,448]{1,2,0:T(8,128)(2,1)}), bf16[16,256,448]{1,2,0:T(8,128)(2,1)}, u32[]{:S(2)}, u32[]{:S(2)}) %all-to-all-start.1) | async-done | bytes 3670048 | tf_op jit(solution)/shard_map/all_to_all | solution.py:40
  158.5 6.4 %stack.2 = bf16[16,896,448]{1,2,0:T(8,128)(2,1)} broadcast(bf16[896,448]{0,1:T(8,128)(2,1)S(1)} %copy.38), dimensions={1,2} | broadcast | bytes 13647872 | tf_op jit(solution)/shard_map/stack | solution.py:11
  164.9 11.1 %all-to-all-start.2 = ((bf16[16,896,448]{1,2,0:T(8,128)(2,1)}), bf16[16,896,448]{1,2,0:T(8,128)(2,1)}, u32[]{:S(2)}, u32[]{:S(2)}) async-start(bf16[16,896,448]{1,2,0:T(8,128)(2,1)} %stack.2), calls=%async_computation.2 | async-start | bytes 25690112 | tf_op jit(solution)/shard_map/all_to_all | solution.py:12
  178.7 177.0 %all-gather.5.cloned.1.call-done = bf16[2,2048,896]{2,1,0:T(8,128)(2,1)} async-done(((bf16[2,128,896]{2,1,0:T(8,128)(2,1)}), bf16[2,2048,896]{2,1,0:T(8,128)(2,1)}) %all-gather.5.cloned.1.call-update) | async-done | bytes 7340048 | tf_op jit(solution)/shard_map/all_gather | solution.py:67
  355.6 6.8 %fusion.49 = (bf16[1,2048,896]{2,1,0:T(8,128)(2,1)}, bf16[1,2048,896]{2,1,0:T(8,128)(2,1)}) fusion(bf16[2,2048,896]{2,1,0:T(8,128)(2,1)} %all-gather.5.cloned.1.call-done), kind=kLoop, calls=%fused_computation.55 | loop fusion | bytes 14680064 | tf_op jit(solution)/shard_map/slice | solution.py:75
  362.5 6.1 %copy.36 = bf16[1,2048,896]{1,2,0:T(8,128)(2,1)} copy(bf16[1,2048,896]{2,1,0:T(8,128)(2,1)} %get-tuple-element.10) | data formatting | bytes 7340032 | tf_op jit(solution)/shard_map/slice | solution.py:75
  368.6 6.2 %copy.37 = bf16[1,2048,896]{1,2,0:T(8,128)(2,1)} copy(bf16[1,2048,896]{2,1,0:T(8,128)(2,1)} %get-tuple-element.11) | data formatting | bytes 7340032 | tf_op jit(solution)/shard_map/slice | solution.py:76
  374.9 9.8 %fusion.23 = bf16[256,896]{1,0:T(8,128)(2,1)S(1)} fusion(bf16[16,896,448]{1,2,0:T(8,128)(2,1)} %all-to-all-done.2, bf16[16,256,448]{1,2,0:T(8,128)(2,1)} %all-to-all-done.1), kind=kOutput, calls=%fused_computation.21 | convolution fusion | flops 3288563712 | bytes 16973824 | tf_op jit(solution)/shard_map/td,hd->th/dot_general | solution.py:41
  384.8 0.4 fusion.51
  385.2 4.0 fusion.2
  389.2 2.2 fusion.3
  391.4 2.1 fusion.10
  393.8 0.4 fusion.28
  394.2 1.0 copy.39
  (25 shorter events, 1.8 us)
Async XLA Ops:
  8.0 93.6 %all-gather.3.cloned.1.call-start = ((), (), s32[]{:S(2)}) async-start(), calls=%async_computation.3 | async-start | bytes 4587520 | tf_op jit(solution)/shard_map/all_gather | solution.py:37
  25.3 80.6 %all-to-all-start = ((bf16[56,16,448]{2,0,1:T(8,128)(2,1)}), bf16[56,16,448]{2,0,1:T(8,128)(2,1)S(1)}, u32[]{:S(2)}, u32[]{:S(2)}) async-start(bf16[56,16,448]{2,0,1:T(8,128)(2,1)} %copy.29), calls=%async_computation | async-start | bytes 1835008 | tf_op jit(solution)/shard_map/all_to_all | solution.py:36
  105.8 52.7 %all-to-all-start.1 = ((bf16[16,256,448]{1,2,0:T(8,128)(2,1)}), bf16[16,256,448]{1,2,0:T(8,128)(2,1)}, u32[]{:S(2)}, u32[]{:S(2)}) async-start(bf16[16,256,448]{1,2,0:T(8,128)(2,1)} %bitcast.79), calls=%async_computation.1 | async-start | bytes 7340032 | tf_op jit(solution)/shard_map/all_to_all | solution.py:40
  111.6 53.3 %copy-start.1 = (bf16[896,448]{0,1:T(8,128)(2,1)}, bf16[896,448]{0,1:T(8,128)(2,1)S(1)}, u32[]{:S(2)}) copy-start(bf16[896,448]{0,1:T(8,128)(2,1)S(1)} %copy.38) | copy-start | bytes 2408452
  164.9 12.3 %copy-start.2 = (bf16[2,256,896]{2,1,0:T(8,128)(2,1)S(1)}, bf16[2,256,896]{2,1,0:T(8,128)(2,1)}, u32[]{:S(2)}) copy-start(bf16[2,256,896]{2,1,0:T(8,128)(2,1)} %param.10) | copy-start | bytes 2752516
  164.9 13.5 %copy-start.3 = (s32[1,64]{1,0:T(1,128)S(1)}, s32[1,64]{1,0:T(1,128)}, u32[]{:S(2)}) copy-start(s32[1,64]{1,0:T(1,128)} %param.11) | copy-start | bytes 772
  164.9 209.9 %all-to-all-start.2 = ((bf16[16,896,448]{1,2,0:T(8,128)(2,1)}), bf16[16,896,448]{1,2,0:T(8,128)(2,1)}, u32[]{:S(2)}, u32[]{:S(2)}) async-start(bf16[16,896,448]{1,2,0:T(8,128)(2,1)} %stack.2), calls=%async_computation.2 | async-start | bytes 25690112 | tf_op jit(solution)/shard_map/all_to_all | solution.py:12
  176.0 179.7 %all-gather.5.cloned.1.call-start = ((), (), s32[]{:S(2)}) async-start(), calls=%async_computation.4 | async-start | bytes 7798784 | tf_op jit(solution)/shard_map/all_gather | solution.py:67
  385.2 6.2 %copy-start = (bf16[1,2048,896]{1,2,0:T(8,128)(2,1)S(1)}, bf16[1,2048,896]{1,2,0:T(8,128)(2,1)}, u32[]{:S(2)}) copy-start(bf16[1,2048,896]{1,2,0:T(8,128)(2,1)} %copy.37) | copy-start | bytes 11010052
Sparse Core Ops, SparseCore 0:
  10.6 90.9 all-gather.2
Sparse Core Ops, SparseCore 1:
  178.2 177.4 all-gather.4
